TPU v7x, 512 devices: a whole 4x8x8 slice. The times are simulated.
512 devices in a mesh: space: 128 (over x, y, z_hi, core), modes: 4 (over z_lo).
Axes of the slice: x: 4, y: 8, z: 8 (z_hi: 2, z_lo: 4; z = z_hi * 4 + z_lo), core: 2. Of those that a mesh axis runs over, the one named last changes fastest.
Arguments:
- voltage_expansion: float32 [220, 128, 2048], P('modes', 'space'), may hold values from -6 to 6
- current_injection: float32 [220, 128, 2048], P('modes', 'space'), may hold values from -48 to 48
- thermal_state: float32 [220, 128, 2048], P('modes', 'space'), may hold values from -6 to 6
- average_electric_transport: float32 [128, 2048], P('space'), may hold values from 0.5 to 4
- material_zone: int32 [128, 2048], P('space'), may hold values from 0 to 3
- zone_relative_response: float32 [4, 9], replicated, may hold values from 0.02 to 0.12
- polynomial_exponent_rows: int32 [220, 9], replicated, may hold values from 0 to 3, as said below
- quadrature_abscissa_choice: int32 [512, 9], replicated, may hold values from 0 to 4
- quadrature_integer_share: int32 [512], replicated, may hold values from 1 to 1024
Outputs:
- relaxed_voltage: float32 [220, 128, 2048], P('modes', 'space')
- advanced_thermal_state: float32 [220, 128, 2048], P('modes', 'space')
Inputs may be any that keep to these rules, and one draw needn't show every extreme that they name: `polynomial_exponent_rows`: the rows are the 220 multi-indices of total degree at most 3 over 9 parameters, each once.
All inputs are finite; a program needn't handle non-finite values.
Results may differ from a plain program's by a relative error of at most 0.0003.
Values sent between devices are 32-bit elements; how exact they have to be, the bound alone decides.
A program may use at most 64 MiB of HBM per device.

v0:
```python
import jax
import jax.numpy as jnp
from jax import lax
from jax.sharding import PartitionSpec as P

NY = 256
NZ = 8
HERMITE_NODES = (
    0.0,
    1.355626179974266,
    -1.355626179974266,
    2.8569700138728056,
    -2.8569700138728056,
)


def padded_2(block, sides, width):
    for axis, dim in sides:
        count = lax.axis_size(axis)
        forward = [(i, i + 1) for i in range(count - 1)]
        backward = [(target, source) for source, target in forward]
        low = lax.ppermute(
            lax.slice_in_dim(block, block.shape[dim] - width, None, axis=dim), axis, forward
        )
        high = lax.ppermute(lax.slice_in_dim(block, 0, width, axis=dim), axis, backward)
        block = jnp.concatenate([low, block, high], axis=dim)
    return block


def neighbours(field):
    column_ids = jnp.arange(field.shape[-1])
    depth_pos = column_ids % NZ
    row_pos = column_ids // NZ
    z_next = jnp.where(depth_pos < NZ - 1, jnp.roll(field, -1, -1), 0.0)
    z_prev = jnp.where(depth_pos > 0, jnp.roll(field, 1, -1), 0.0)
    y_next = jnp.where(row_pos < NY - 1, jnp.roll(field, -NZ, -1), 0.0)
    y_prev = jnp.where(row_pos > 0, jnp.roll(field, NZ, -1), 0.0)
    return (z_next, z_prev, y_next, y_prev)


def diffusion_operator_weights(padded):
    center = padded[..., 1:-1, :]
    z_next, z_prev, y_next, y_prev = neighbours(center)
    return (
        6.0 * center - padded[..., 2:, :] - padded[..., :-2, :] - z_next - z_prev - y_next - y_prev
    )


def gradient(padded):
    center = padded[..., 1:-1, :]
    z_next, z_prev, y_next, y_prev = neighbours(center)
    along_x = (padded[..., 2:, :] - padded[..., :-2, :]) * 0.5
    along_y = (y_next - y_prev) * 0.5
    along_z = (z_next - z_prev) * 0.5
    return jnp.stack([along_x, along_y, along_z])


def coupling(row_table, col_table):
    offsets = row_table[:, None, :] - col_table[None, :, :]
    differ_count = jnp.sum((offsets != 0).astype(jnp.int32), axis=2)
    layers = [jnp.where(differ_count == 0, 1.0, 0.0).astype(jnp.float32)]
    for which_param in range(row_table.shape[1]):
        larger = jnp.maximum(
            row_table[:, None, which_param], col_table[None, :, which_param]
        ).astype(jnp.float32)
        linked = (jnp.abs(offsets[:, :, which_param]) == 1) & (differ_count == 1)
        layers.append(jnp.where(linked, jnp.sqrt(larger), 0.0))
    return jnp.stack(layers)


def node_values(quadrature_abscissa_choice):
    node_vals = jnp.zeros(quadrature_abscissa_choice.shape, jnp.float32)
    for which_node in range(5):
        node_vals = node_vals + jnp.where(
            quadrature_abscissa_choice == which_node, HERMITE_NODES[which_node], 0.0
        )
    return node_vals


def basis_values(polynomial_exponent_rows, node_vals):
    poly_terms = [
        jnp.ones_like(node_vals),
        node_vals,
        (node_vals * node_vals - 1.0) / jnp.sqrt(2.0),
        (node_vals * node_vals * node_vals - 3.0 * node_vals) / jnp.sqrt(6.0),
    ]
    basis_vals = jnp.ones((node_vals.shape[0], polynomial_exponent_rows.shape[0]), jnp.float32)
    for which_param in range(polynomial_exponent_rows.shape[1]):
        degree = polynomial_exponent_rows[:, which_param]
        factor = jnp.zeros_like(basis_vals)
        for which_deg in range(4):
            factor = factor + jnp.where(
                degree[None, :] == which_deg, poly_terms[which_deg][:, which_param][:, None], 0.0
            )
        basis_vals = basis_vals * factor
    return basis_vals


def on_device(
    voltage_expansion,
    current_injection,
    thermal_state,
    average_electric_transport,
    material_zone,
    zone_relative_response,
    polynomial_exponent_rows,
    quadrature_abscissa_choice,
    quadrature_integer_share,
):
    hp = lax.Precision.HIGHEST
    modes_here = voltage_expansion.shape[0]
    planes = voltage_expansion.shape[1]
    columns = voltage_expansion.shape[2]
    cell_count = planes * columns
    nreg = zone_relative_response.shape[0]
    all_modes = polynomial_exponent_rows.shape[0]
    num_points = quadrature_integer_share.shape[0]
    first_mode = lax.axis_index("modes") * modes_here
    own_table = lax.dynamic_slice_in_dim(polynomial_exponent_rows, first_mode, modes_here, 0)
    bordered_quantities = padded_2(
        jnp.stack([voltage_expansion, thermal_state]), (("space", 2),), 1
    )
    pot_padded = bordered_quantities[0]
    thermal_state_bordered = bordered_quantities[1]
    sens_cell = jnp.zeros((zone_relative_response.shape[1],) + material_zone.shape, jnp.float32)
    for which_region in range(nreg):
        sens_cell = sens_cell + jnp.where(
            material_zone[None] == which_region,
            zone_relative_response[which_region][:, None, None],
            0.0,
        )
    coeff = (
        jnp.concatenate([jnp.ones((1,) + material_zone.shape, jnp.float32), sens_cell])
        * average_electric_transport
    )
    coeff_flat = coeff.reshape(coeff.shape[0], cell_count)
    flat_rough = diffusion_operator_weights(pot_padded).reshape(modes_here, cell_count)
    row_coup = coupling(own_table, polynomial_exponent_rows)
    mixed = jnp.einsum(
        "mij,jc->mic",
        row_coup,
        lax.all_gather(flat_rough, "modes", axis=0, tiled=True),
        precision=hp,
    )
    applied = jnp.sum(coeff_flat[:, None, :] * mixed, axis=0)
    applied = applied.reshape(modes_here, planes, columns)
    relaxed_voltage = voltage_expansion + 0.8 * (current_injection - applied) / (
        6.0 * average_electric_transport
    )
    node_vals = node_values(quadrature_abscissa_choice)
    basis_vals = basis_values(polynomial_exponent_rows, node_vals)
    new_padded = padded_2(relaxed_voltage, (("space", 1),), 1)
    grads = gradient(new_padded)
    point_grads = jnp.einsum(
        "qi,kixn->kqxn",
        basis_vals,
        lax.all_to_all(grads, "modes", split_axis=3, concat_axis=1, tiled=True),
        precision=hp,
    )
    quarter = columns // lax.axis_size("modes")
    offset = lax.axis_index("modes") * quarter
    cond_part = lax.dynamic_slice_in_dim(average_electric_transport, offset, quarter, 1)
    region_part = lax.dynamic_slice_in_dim(material_zone, offset, quarter, 1)
    cond_lift = 1.0 + jnp.dot(zone_relative_response, node_vals.T, precision=hp)
    spread = jnp.zeros((num_points, planes, quarter), jnp.float32)
    for which_region in range(nreg):
        spread = spread + jnp.where(
            region_part[None] == which_region, cond_lift[which_region][:, None, None], 0.0
        )
    joule_heat = cond_part * spread * jnp.sum(point_grads * point_grads, axis=0)
    weighted = (
        basis_vals.T
        * quadrature_integer_share[None, :].astype(jnp.float32)
        / (512.0 * num_points * all_modes)
    )
    heat_points = jnp.einsum("iq,qxn->ixn", weighted, joule_heat, precision=hp)
    thermal_expansion_terms = lax.all_to_all(
        heat_points, "modes", split_axis=0, concat_axis=2, tiled=True
    )
    advanced_thermal_state = thermal_state + 0.1 * (
        thermal_expansion_terms - 1.5 * diffusion_operator_weights(thermal_state_bordered)
    )
    return (relaxed_voltage, advanced_thermal_state)


def solution(mesh):
    in_specs = (
        P("modes", "space", None),
        P("modes", "space", None),
        P("modes", "space", None),
        P("space", None),
        P("space", None),
        P(),
        P(),
        P(),
        P(),
    )
    out_specs = (P("modes", "space", None), P("modes", "space", None))
    return jax.shard_map(
        on_device, mesh=mesh, in_specs=in_specs, out_specs=out_specs, check_vma=False
    )
```

profile of v0, /device:TPU:59, one launch (start us, length us, event | category | flops | bytes accessed | tf_op | source)
XLA Modules:
  0.0 265.5 jit_solution(5457627602112726379)
XLA Ops:
  7.2 1.4 copy_bitcast_fusion
  8.8 0.7 copy.62
  9.5 2.6 collective-permute-start.1
  12.1 10.5 %collective-permute-start = (f32[2,55,1,2048]{3,0,2,1:T(2,128)S(1)}, f32[2,55,1,2048]{3,0,2,1:T(2,128)}, u32[]{:S(2)}, u32[]{:S(2)}) collective-permute-start(f32[2,55,1,2048]{3,0,2,1:T(2,128)S(1)} %copy.62), channel_id=1, source_target_pairs={{0,4},{4,8},{8,12},{12,16},{16,20},{20,24},{24,28},{28,32},{32,36}... | collective-permute-start | bytes 2703368 | tf_op jit(solution)/shard_map/ppermute | solution.py:22
  22.9 0.1 broadcast_subtract_fusion
  23.0 0.6 bitcast_dynamic-update-slice_fusion
  23.8 0.6 compare_reduce_fusion.7
  24.5 0.7 select_dynamic-update-slice_fusion.8
  25.2 0.7 select_dynamic-update-slice_fusion.7
  25.9 0.7 select_dynamic-update-slice_fusion.6
  26.7 0.7 select_dynamic-update-slice_fusion.5
  27.4 27.7 %collective-permute-done.1 = f32[2,55,1,2048]{3,0,2,1:T(2,128)} collective-permute-done((f32[2,55,1,2048]{3,0,2,1:T(2,128)S(1)}, f32[2,55,1,2048]{3,0,2,1:T(2,128)}, u32[]{:S(2)}, u32[]{:S(2)}) %collective-permute-start.1) | collective-permute-done | bytes 901152 | tf_op jit(solution)/shard_map/ppermute | solution.py:25
  55.0 1.7 copy.65
  56.7 8.6 %collective-permute-done = f32[2,55,1,2048]{3,0,2,1:T(2,128)} collective-permute-done((f32[2,55,1,2048]{3,0,2,1:T(2,128)S(1)}, f32[2,55,1,2048]{3,0,2,1:T(2,128)}, u32[]{:S(2)}, u32[]{:S(2)}) %collective-permute-start) | collective-permute-done | bytes 901152 | tf_op jit(solution)/shard_map/ppermute | solution.py:22
  65.4 1.7 copy.64
  67.1 0.3 pad_maximum_fusion
  67.3 0.2 slice_bitcast_fusion
  67.6 0.2 fusion.347
  67.9 0.2 fusion.345
  68.1 0.4 fusion.32
  68.5 1.2 copy.66
  69.8 0.5 broadcast_compare_fusion.27
  70.3 0.7 select_dynamic-update-slice_fusion.4
  71.1 0.7 select_dynamic-update-slice_fusion.3
  71.8 0.7 select_dynamic-update-slice_fusion.2
  72.5 0.7 select_dynamic-update-slice_fusion.1
  73.2 0.7 select_dynamic-update-slice_fusion
  73.9 0.1 select_add_fusion
  74.1 42.7 %all-gather.3.cloned.1.call-done = f32[220,1,2048]{2,1,0:T(1,128)} async-done(((f32[55,1,2048]{2,1,0:T(1,128)}), f32[220,1,2048]{2,1,0:T(1,128)}) %all-gather.3.cloned.1.call-update) | async-done | bytes 1802256 | tf_op jit(solution)/shard_map/all_gather | solution.py:142
  116.8 5.9 %multiply_reduce_fusion = f32[55,2048]{1,0:T(8,128)S(1)} fusion(f32[10,55,220]{2,1,0:T(8,128)} %select_dynamic-update-slice_fusion, f32[10,2048]{1,0:T(8,128)S(1)} %multiply_bitcast_fusion.1, f32[220,1,2048]{2,1,0:T(1,128)} %all-gather.3.cloned.1.call-done), kind=kOutput, calls=%fused_computation | convolution fusion | flops 2975836160 | bytes 2818720 | tf_op jit(solution)/shard_map/mij,jc->mic/dot_general | solution.py:139
  122.8 0.4 fusion.40
  123.2 0.2 slice_bitcast_fusion.2
  123.5 0.2 slice_bitcast_fusion.4
  123.7 3.1 %collective-permute-start.2 = (f32[55,1,2048]{2,0,1:T(8,128)S(1)}, f32[55,1,2048]{2,0,1:T(8,128)S(1)}, u32[]{:S(2)}, u32[]{:S(2)}) collective-permute-start(f32[55,1,2048]{2,0,1:T(8,128)S(1)} %fusion.40), channel_id=1, source_target_pairs={{4,0},{8,4},{12,8},{16,12},{20,16},{24,20},{28,24},{32,28},{36,32}... | collective-permute-start | bytes 1351688 | tf_op jit(solution)/shard_map/ppermute | solution.py:25
  126.8 6.6 %collective-permute-start.3 = (f32[55,1,2048]{2,0,1:T(8,128)S(1)}, f32[55,1,2048]{2,0,1:T(8,128)S(1)}, u32[]{:S(2)}, u32[]{:S(2)}) collective-permute-start(f32[55,1,2048]{2,0,1:T(8,128)S(1)} %fusion.40), channel_id=1, source_target_pairs={{0,4},{4,8},{8,12},{12,16},{16,20},{20,24},{24,28},{28,32},{32,36}... | collective-permute-start | bytes 1351688 | tf_op jit(solution)/shard_map/ppermute | solution.py:22
  133.3 0.2 fusion.36
  133.5 0.2 fusion.34
  133.7 9.7 %collective-permute-done.2 = f32[55,1,2048]{2,0,1:T(8,128)S(1)} collective-permute-done((f32[55,1,2048]{2,0,1:T(8,128)S(1)}, f32[55,1,2048]{2,0,1:T(8,128)S(1)}, u32[]{:S(2)}, u32[]{:S(2)}) %collective-permute-start.2) | collective-permute-done | bytes 450592 | tf_op jit(solution)/shard_map/ppermute | solution.py:25
  143.4 11.2 %collective-permute-done.3 = f32[55,1,2048]{2,0,1:T(8,128)S(1)} collective-permute-done((f32[55,1,2048]{2,0,1:T(8,128)S(1)}, f32[55,1,2048]{2,0,1:T(8,128)S(1)}, u32[]{:S(2)}, u32[]{:S(2)}) %collective-permute-start.3) | collective-permute-done | bytes 450592 | tf_op jit(solution)/shard_map/ppermute | solution.py:22
  154.8 3.1 %copy.71 = f32[3,55,1,2048]{1,0,2,3:T(4,128)} copy(f32[3,55,1,2048]{3,1,2,0:T(8,128)S(1)} %pad_maximum_fusion.1) | data formatting | bytes 2703360 | tf_op jit(solution)/shard_map/stack | solution.py:55
  157.9 6.6 %reshape.2106 = f32[4,1,84480]{2,1,0:T(1,128)} reshape(f32[2048,1,3,55]{3,2,1,0:T(4,128)} %bitcast.196) | data formatting | bytes 2703360
  164.6 3.7 %all-to-all-start = ((f32[4,1,84480]{2,1,0:T(1,128)}), f32[4,1,84480]{2,1,0:T(1,128)S(1)}, u32[]{:S(2)}, u32[]{:S(2)}) async-start(f32[4,1,84480]{2,1,0:T(1,128)} %reshape.2106), calls=%async_computation | async-start | bytes 2703360 | tf_op jit(solution)/shard_map/all_to_all | solution.py:157
  168.3 0.2 fusion.2
  168.6 1.1 fusion.343
  169.7 29.8 %all-to-all-done = f32[4,1,84480]{2,1,0:T(1,128)S(1)} async-done(((f32[4,1,84480]{2,1,0:T(1,128)}), f32[4,1,84480]{2,1,0:T(1,128)S(1)}, u32[]{:S(2)}, u32[]{:S(2)}) %all-to-all-start) | async-done | bytes 1351712 | tf_op jit(solution)/shard_map/all_to_all | solution.py:157
  199.6 0.5 broadcast.1558
  200.1 5.6 %reduce.20 = f32[4,84480]{1,0:T(4,128)} reduce(f32[4,1,84480]{2,1,0:T(1,128)S(1)} %all-to-all-done, f32[]{:T(128)} %broadcast.1558), dimensions={1}, to_apply=%all_to_all.24.reduce_sub_computation | reduce | bytes 2703364 | tf_op jit(solution)/shard_map/all_to_all | solution.py:157
  205.7 6.9 %reshape.2107 = f32[2048,1,3,55]{3,2,1,0:T(4,128)} reshape(f32[4,84480]{1,0:T(4,128)} %reduce.20) | data formatting | bytes 2703360
  212.6 4.6 %copy.79 = f32[3,55,1,4,512]{4,3,1,0,2:T(4,128)} copy(f32[3,55,1,4,512]{1,0,4,3,2:T(4,128)} %bitcast.197) | data formatting | bytes 2703360 | tf_op jit(solution)/shard_map/all_to_all | solution.py:157
  217.2 1.8 copy.73
  219.0 1.3 reshape.2092
  220.3 6.3 %multiply_reduce_fusion.1 = f32[512,512]{1,0:T(8,128)S(1)} fusion(f32[3,220,512]{2,1,0:T(8,128)} %reshape.2092, f32[512]{0:T(512)S(1)} %bitcast.231, f32[512]{0:T(512)S(1)} %bitcast.279, f32[512]{0:T(512)S(1)} %bitcast.259, f32[220]{0:T(256)S(1)} %get-tuple-element.133, f32[512]{0:T(512)S(1)} %bitcast.233, f32[512]{0:T(512)S(1)} %bitcast.277, ...), kind=kOutput, calls=%fused_computation.1 | convolution fusion | flops 2084474880 | bytes 2469412 | tf_op jit(solution)/shard_map/qi,kixn->kqxn/dot_general | solution.py:154
  226.6 3.1 %convolution_bitcast_fusion = f32[220,1,512]{2,0,1:T(8,128)S(1)} fusion(f32[512,512]{1,0:T(8,128)S(1)} %multiply_reduce_fusion.1, f32[512]{0:T(512)S(1)} %bitcast.285, f32[512]{0:T(512)S(1)} %bitcast.286, f32[512]{0:T(512)S(1)} %bitcast.287, f32[512]{0:T(512)S(1)} %bitcast.284, f32[512]{0:T(512)S(1)} %bitcast.283, pred[512]{0:T(512)(128)(4,1)S(1)} %copy-done.13, ...), kind=kOutput, calls=%fused_computation.8 | convolution fusion | flops 701628416 | bytes 1582628 | tf_op jit(solution)/shard_map/iq,qxn->ixn/dot_general | solution.py:176
  229.7 1.2 copy.74
  230.9 3.7 %all-to-all-start.1 = ((f32[220,1,512]{2,1,0:T(1,128)}), f32[220,1,512]{2,1,0:T(1,128)S(1)}, u32[]{:S(2)}, u32[]{:S(2)}) async-start(f32[220,1,512]{2,1,0:T(1,128)} %copy.74), calls=%async_computation.1 | async-start | bytes 901120 | tf_op jit(solution)/shard_map/all_to_all | solution.py:177
  234.7 0.2 fusion.341
  234.9 1.2 copy.77
  236.2 11.5 %all-to-all-done.1 = f32[220,1,512]{2,1,0:T(1,128)S(1)} async-done(((f32[220,1,512]{2,1,0:T(1,128)}), f32[220,1,512]{2,1,0:T(1,128)S(1)}, u32[]{:S(2)}, u32[]{:S(2)}) %all-to-all-start.1) | async-done | bytes 450592 | tf_op jit(solution)/shard_map/all_to_all | solution.py:177
  247.7 1.9 reduce.11
  249.6 1.9 all_to_all.28
  251.6 2.1 copy.75
  253.6 2.1 all_to_all.30
  255.7 1.7 fusion.28
  257.4 1.2 copy.78
  (69 shorter events, 1.3 us)
Async XLA Ops:
  7.2 109.7 %all-gather.3.cloned.1.call-start = ((), (), s32[]{:S(2)}) async-start(), calls=%async_computation.2 | async-start | bytes 2252800 | tf_op jit(solution)/shard_map/all_gather | solution.py:142
  8.7 14.0 %copy-start.4 = (s32[220,9]{0,1:T(8,128)S(1)}, s32[220,9]{0,1:T(8,128)}, u32[]{:S(2)}) copy-start(s32[220,9]{0,1:T(8,128)} %param.15) | copy-start | bytes 23764
  8.7 14.9 %copy-start.7 = (s32[1,2048]{1,0:T(1,128)S(1)}, s32[1,2048]{1,0:T(1,128)}, u32[]{:S(2)}) copy-start(s32[1,2048]{1,0:T(1,128)} %param.13) | copy-start | bytes 24580
  8.8 15.6 %copy-start.5 = (f32[1,2048]{1,0:T(1,128)S(1)}, f32[1,2048]{1,0:T(1,128)}, u32[]{:S(2)}) copy-start(f32[1,2048]{1,0:T(1,128)} %param.12) | copy-start | bytes 24580
  8.8 15.6 %copy-start.8 = (s32[512]{0:T(512)S(1)}, s32[512]{0:T(512)}, u32[]{:S(2)}) copy-start(s32[512]{0:T(512)} %param.17) | copy-start | bytes 6148
  8.8 16.4 %copy-start.9 = (f32[4,9]{1,0:T(4,128)S(1)}, f32[4,9]{1,0:T(4,128)}, u32[]{:S(2)}) copy-start(f32[4,9]{1,0:T(4,128)} %param.14) | copy-start | bytes 436
  9.5 45.6 %collective-permute-start.1 = (f32[2,55,1,2048]{3,0,2,1:T(2,128)S(1)}, f32[2,55,1,2048]{3,0,2,1:T(2,128)}, u32[]{:S(2)}, u32[]{:S(2)}) collective-permute-start(f32[2,55,1,2048]{3,0,2,1:T(2,128)S(1)} %copy.62), channel_id=1, source_target_pairs={{4,0},{8,4},{12,8},{16,12},{20,16},{24,20},{28,24},{32,28},{36,32}... | collective-permute-start | bytes 2703368 | tf_op jit(solution)/shard_map/ppermute | solution.py:25
  12.1 53.3 %collective-permute-start = (f32[2,55,1,2048]{3,0,2,1:T(2,128)S(1)}, f32[2,55,1,2048]{3,0,2,1:T(2,128)}, u32[]{:S(2)}, u32[]{:S(2)}) collective-permute-start(f32[2,55,1,2048]{3,0,2,1:T(2,128)S(1)} %copy.62), channel_id=1, source_target_pairs={{0,4},{4,8},{8,12},{12,16},{16,20},{20,24},{24,28},{28,32},{32,36}... | collective-permute-start | bytes 2703368 | tf_op jit(solution)/shard_map/ppermute | solution.py:22
  74.1 48.7 %copy-start.2 = (f32[55,1,2048]{2,1,0:T(1,128)S(1)}, f32[55,1,2048]{2,1,0:T(1,128)}, u32[]{:S(2)}) copy-start(f32[55,1,2048]{2,1,0:T(1,128)} %param.9) | copy-start | bytes 1351684
  74.1 48.7 %copy-start.3 = (f32[55,1,2048]{2,1,0:T(1,128)S(1)}, f32[55,1,2048]{2,1,0:T(1,128)}, u32[]{:S(2)}) copy-start(f32[55,1,2048]{2,1,0:T(1,128)} %param.10) | copy-start | bytes 1351684
  123.7 19.7 %collective-permute-start.2 = (f32[55,1,2048]{2,0,1:T(8,128)S(1)}, f32[55,1,2048]{2,0,1:T(8,128)S(1)}, u32[]{:S(2)}, u32[]{:S(2)}) collective-permute-start(f32[55,1,2048]{2,0,1:T(8,128)S(1)} %fusion.40), channel_id=1, source_target_pairs={{4,0},{8,4},{12,8},{16,12},{20,16},{24,20},{28,24},{32,28},{36,32}... | collective-permute-start | bytes 1351688 | tf_op jit(solution)/shard_map/ppermute | solution.py:25
  126.8 27.9 %collective-permute-start.3 = (f32[55,1,2048]{2,0,1:T(8,128)S(1)}, f32[55,1,2048]{2,0,1:T(8,128)S(1)}, u32[]{:S(2)}, u32[]{:S(2)}) collective-permute-start(f32[55,1,2048]{2,0,1:T(8,128)S(1)} %fusion.40), channel_id=1, source_target_pairs={{0,4},{4,8},{8,12},{12,16},{16,20},{20,24},{24,28},{28,32},{32,36}... | collective-permute-start | bytes 1351688 | tf_op jit(solution)/shard_map/ppermute | solution.py:22
  164.6 3.7 %copy-start.6 = (s32[512,9]{0,1:T(8,128)S(1)}, s32[512,9]{0,1:T(8,128)}, u32[]{:S(2)}) copy-start(s32[512,9]{0,1:T(8,128)} %param.16) | copy-start | bytes 55300
  164.6 35.0 %all-to-all-start = ((f32[4,1,84480]{2,1,0:T(1,128)}), f32[4,1,84480]{2,1,0:T(1,128)S(1)}, u32[]{:S(2)}, u32[]{:S(2)}) async-start(f32[4,1,84480]{2,1,0:T(1,128)} %reshape.2106), calls=%async_computation | async-start | bytes 2703360 | tf_op jit(solution)/shard_map/all_to_all | solution.py:157
  220.2 6.3 %copy-start.10 = (pred[512]{0:T(512)(128)(4,1)S(1)}, pred[512]{0:T(512)(128)(4,1)}, u32[]{:S(2)}) copy-start(pred[512]{0:T(512)(128)(4,1)} %get-tuple-element.12) | copy-start | bytes 1540
  220.2 6.3 %copy-start.11 = (pred[512]{0:T(512)(128)(4,1)S(1)}, pred[512]{0:T(512)(128)(4,1)}, u32[]{:S(2)}) copy-start(pred[512]{0:T(512)(128)(4,1)} %get-tuple-element.13) | copy-start | bytes 1540
  220.3 6.3 %copy-start.12 = (pred[512]{0:T(512)(128)(4,1)S(1)}, pred[512]{0:T(512)(128)(4,1)}, u32[]{:S(2)}) copy-start(pred[512]{0:T(512)(128)(4,1)} %get-tuple-element.14) | copy-start | bytes 1540
  220.3 6.3 %copy-start.13 = (pred[512]{0:T(512)(128)(4,1)S(1)}, pred[512]{0:T(512)(128)(4,1)}, u32[]{:S(2)}) copy-start(pred[512]{0:T(512)(128)(4,1)} %get-tuple-element.15) | copy-start | bytes 1540
  220.3 6.3 %copy-start.14 = (pred[220]{0:T(512)(128)(4,1)S(1)}, pred[220]{0:T(512)(128)(4,1)}, u32[]{:S(2)}) copy-start(pred[220]{0:T(512)(128)(4,1)} %get-tuple-element.106) | copy-start | bytes 664
  220.3 6.3 %copy-start.15 = (pred[220]{0:T(512)(128)(4,1)S(1)}, pred[220]{0:T(512)(128)(4,1)}, u32[]{:S(2)}) copy-start(pred[220]{0:T(512)(128)(4,1)} %get-tuple-element.107) | copy-start | bytes 664
  220.3 6.3 %copy-start.16 = (pred[220]{0:T(512)(128)(4,1)S(1)}, pred[220]{0:T(512)(128)(4,1)}, u32[]{:S(2)}) copy-start(pred[220]{0:T(512)(128)(4,1)} %get-tuple-element.108) | copy-start | bytes 664
  230.9 16.8 %all-to-all-start.1 = ((f32[220,1,512]{2,1,0:T(1,128)}), f32[220,1,512]{2,1,0:T(1,128)S(1)}, u32[]{:S(2)}, u32[]{:S(2)}) async-start(f32[220,1,512]{2,1,0:T(1,128)} %copy.74), calls=%async_computation.1 | async-start | bytes 901120 | tf_op jit(solution)/shard_map/all_to_all | solution.py:177
  249.6 6.1 %copy-start = (f32[55,1,2047]{2,0,1:T(8,128)S(1)}, f32[55,1,2047]{2,0,1:T(8,128)}, u32[]{:S(2)}) copy-start(f32[55,1,2047]{2,0,1:T(8,128)} %get-tuple-element.30) | copy-start | bytes 1351024
  249.6 6.1 %copy-start.1 = (f32[55,1,2047]{2,0,1:T(8,128)S(1)}, f32[55,1,2047]{2,0,1:T(8,128)}, u32[]{:S(2)}) copy-start(f32[55,1,2047]{2,0,1:T(8,128)} %get-tuple-element.31) | copy-start | bytes 1351024
Sparse Core Ops, SparseCore 0:
  69.9 46.8 all-gather.2
where the time goes:
time: 266 us
  waiting for transfers between devices  141 us (53%)
  local copies, waits for them, and re-layouts  44.4 us (17%)
  starting transfers between devices  30.2 us (11%)
  other arithmetic  19.7 us (7%)
  matrix products  15.4 us (6%)
  between operations  14.5 us (5%)
    all_gather x1, waiting for transfers between devices, on_device(): lax.all_gather(flat_rough, 'modes', axis=0, tiled=True)  42.7 us
    ppermute x2, waiting for transfers between devices, padded_2(): lax.ppermute(lax.slice_in_dim(block, 0, width, axis=dim), axis, backward)  37.3 us
    all_to_all x1, waiting for transfers between devices, on_device(): lax.all_to_all(grads, 'modes', split_axis=3, concat_axis=1, tiled=True)  29.8 us
    ppermute x2, waiting for transfers between devices, padded_2(): lax.ppermute(lax.slice_in_dim(block, block.shape[dim] - width, None, axis...  19.9 us
    unnamed x39, local copies, waits for them, and re-layouts  17.5 us
    ppermute x2, starting transfers between devices, padded_2(): lax.ppermute(lax.slice_in_dim(block, block.shape[dim] - width, None, axis...  17.1 us
    all_to_all x1, waiting for transfers between devices, on_device(): lax.all_to_all(heat_points, 'modes', split_axis=0, concat_axis=2, tiled=T...  11.5 us
    all_to_all x3, local copies, waits for them, and re-layouts, on_device(): lax.all_to_all(grads, 'modes', split_axis=3, concat_axis=1, tiled=True)  6.9 us
  transfers between devices with their start and end apart: 7, of which 7 were waited for; matrix products, arithmetic and copies ran while one was open for 5% of the time, Pallas kernels for 0%

commit v1 on v0

--- a/solution.py
+++ b/solution.py
@@ -11,6 +11,15 @@
     -1.355626179974266,
     2.8569700138728056,
     -2.8569700138728056,
+)
+note_pipes_for = lambda which_axis, mine_x: jnp.concatenate(
+    lax.all_to_all(
+        jnp.stack(jnp.split(mine_x, lax.axis_size(which_axis), axis=3)),
+        axis_name=which_axis,
+        split_axis=0,
+        concat_axis=0,
+    ),
+    axis=1,
 )
 
 
@@ -152,10 +161,7 @@
     new_padded = padded_2(relaxed_voltage, (("space", 1),), 1)
     grads = gradient(new_padded)
     point_grads = jnp.einsum(
-        "qi,kixn->kqxn",
-        basis_vals,
-        lax.all_to_all(grads, "modes", split_axis=3, concat_axis=1, tiled=True),
-        precision=hp,
+        "qi,kixn->kqxn", basis_vals, note_pipes_for("modes", grads), precision=hp
     )
     quarter = columns // lax.axis_size("modes")
     offset = lax.axis_index("modes") * quarter

time: 266 us -> 246 us (0.925)
  local copies, waits for them, and re-layouts: 44.4 us -> 24.7 us
    ppermute x2, waiting for transfers between devices: 37.3 us -> 5.25 us  [padded_2(): lax.ppermute(lax.slice_in_dim(block, 0, width, axis=dim), axis, backward)]
    ppermute x2, waiting for transfers between devices: 19.9 us -> 45.1 us  [padded_2(): lax.ppermute(lax.slice_in_dim(block, block.shape[dim] - width, None, axis...]
    unnamed x39 -> x38, local copies, waits for them, and re-layouts: 17.5 us -> 3.85 us
    all_to_all x3 -> x0, local copies, waits for them, and re-layouts: 6.9 us -> none  [on_device(): lax.all_to_all(grads, 'modes', split_axis=3, concat_axis=1, tiled=True)]
    all_to_all x1 -> x0, other arithmetic: 5.65 us -> none  [on_device(): lax.all_to_all(grads, 'modes', split_axis=3, concat_axis=1, tiled=True)]
    all_gather x1, waiting for transfers between devices: 42.7 us -> 46 us  [on_device(): lax.all_gather(flat_rough, 'modes', axis=0, tiled=True)]
  transfers between devices with their start and end apart: 7 -> 7, of which waited for: 7 -> 6; matrix products, arithmetic and copies ran while one was open for 5% -> 7% of each run, Pallas kernels for 0% -> 0%
where the time goes in v1:
time: 246 us; the launch traced here: 245 us
  waiting for transfers between devices  139 us (57%)
  starting transfers between devices  30.4 us (12%)
  local copies, waits for them, and re-layouts  24.7 us (10%)
  other arithmetic  21 us (9%)
  matrix products  15.4 us (6%)
  between operations  14.6 us (6%)
    all_gather x1, waiting for transfers between devices, on_device(): lax.all_gather(flat_rough, 'modes', axis=0, tiled=True)  46 us
    ppermute x2, waiting for transfers between devices, padded_2(): lax.ppermute(lax.slice_in_dim(block, block.shape[dim] - width, None, axis...  45.1 us
    all_to_all x1, waiting for transfers between devices, lax.all_to_all(jnp.stack(jnp.split(mine_x, lax.axis_size(which_axis), axi...  29.9 us
    ppermute x2, starting transfers between devices, padded_2(): lax.ppermute(lax.slice_in_dim(block, block.shape[dim] - width, None, axis...  17.8 us
    all_to_all x1, waiting for transfers between devices, on_device(): lax.all_to_all(heat_points, 'modes', split_axis=0, concat_axis=2, tiled=T...  12.8 us
    unnamed x9, other arithmetic  6.35 us
    dot_general x1, matrix products, on_device(): jnp.einsum('qi,kixn->kqxn', basis_vals, note_pipes_for('modes', grads), p...  6.25 us
    all_to_all x3, local copies, waits for them, and re-layouts, on_device(): lax.all_to_all(heat_points, 'modes', split_axis=0, concat_axis=2, tiled=T...  6.07 us
  transfers between devices with their start and end apart: 7, of which 6 were waited for; matrix products, arithmetic and copies ran while one was open for 7% of the time, Pallas kernels for 0%

profile of v1, /device:TPU:59, one launch (start us, length us, event | category | flops | bytes accessed | tf_op | source)
XLA Modules:
  0.0 245.1 jit_solution(8144154023790402048)
XLA Ops:
  7.2 1.4 copy_bitcast_fusion
  8.8 0.7 copy.34
  9.5 11.2 %collective-permute-start = (f32[2,55,1,2048]{3,0,2,1:T(2,128)S(1)}, f32[2,55,1,2048]{3,0,2,1:T(2,128)}, u32[]{:S(2)}, u32[]{:S(2)}) collective-permute-start(f32[2,55,1,2048]{3,0,2,1:T(2,128)S(1)} %copy.34), channel_id=1, source_target_pairs={{0,4},{4,8},{8,12},{12,16},{16,20},{20,24},{24,28},{28,32},{32,36}... | collective-permute-start | bytes 2703368 | tf_op jit(solution)/shard_map/ppermute | solution.py:31
  20.7 1.9 collective-permute-start.1
  22.9 0.1 broadcast_subtract_fusion
  23.0 0.6 bitcast_dynamic-update-slice_fusion
  23.8 0.6 compare_reduce_fusion.7
  24.4 0.1 dynamic-slice_bitcast_fusion
  24.5 0.7 select_dynamic-update-slice_fusion.8
  25.2 0.7 select_dynamic-update-slice_fusion.7
  25.9 0.7 select_dynamic-update-slice_fusion.6
  26.7 0.7 select_dynamic-update-slice_fusion.5
  27.4 33.9 %collective-permute-done = f32[2,55,1,2048]{3,0,2,1:T(2,128)} collective-permute-done((f32[2,55,1,2048]{3,0,2,1:T(2,128)S(1)}, f32[2,55,1,2048]{3,0,2,1:T(2,128)}, u32[]{:S(2)}, u32[]{:S(2)}) %collective-permute-start) | collective-permute-done | bytes 901152 | tf_op jit(solution)/shard_map/ppermute | solution.py:31
  61.3 1.7 copy.36
  63.0 1.7 copy.37
  64.7 0.3 pad_maximum_fusion
  65.0 0.2 slice_bitcast_fusion
  65.2 0.2 fusion.342
  65.4 0.2 fusion.344
  65.7 0.5 fusion.32
  66.2 1.2 copy.38
  67.4 0.5 broadcast_compare_fusion.27
  68.0 0.7 select_dynamic-update-slice_fusion.4
  68.7 0.7 select_dynamic-update-slice_fusion.3
  69.4 0.7 select_dynamic-update-slice_fusion.2
  70.1 0.7 select_dynamic-update-slice_fusion.1
  70.8 0.7 select_dynamic-update-slice_fusion
  71.6 0.1 select_add_fusion
  71.7 46.0 %all-gather.3.cloned.1.call-done = f32[220,1,2048]{2,1,0:T(1,128)} async-done(((f32[55,1,2048]{2,1,0:T(1,128)}), f32[220,1,2048]{2,1,0:T(1,128)}) %all-gather.3.cloned.1.call-update) | async-done | bytes 1802256 | tf_op jit(solution)/shard_map/all_gather | solution.py:151
  117.8 5.9 %multiply_reduce_fusion = f32[55,2048]{1,0:T(8,128)S(1)} fusion(f32[10,55,220]{2,1,0:T(8,128)} %select_dynamic-update-slice_fusion, f32[10,2048]{1,0:T(8,128)S(1)} %multiply_bitcast_fusion.1, f32[220,1,2048]{2,1,0:T(1,128)} %all-gather.3.cloned.1.call-done), kind=kOutput, calls=%fused_computation | convolution fusion | flops 2975836160 | bytes 2818720 | tf_op jit(solution)/shard_map/mij,jc->mic/dot_general | solution.py:148
  123.7 0.9 divide_add_fusion
  124.6 3.1 %collective-permute-start.2 = (f32[55,1,2048]{2,1,0:T(1,128)S(1)}, f32[55,1,2048]{2,1,0:T(1,128)S(1)}, u32[]{:S(2)}, u32[]{:S(2)}) collective-permute-start(f32[55,1,2048]{2,1,0:T(1,128)S(1)} %divide_add_fusion), channel_id=1, source_target_pairs={{4,0},{8,4},{12,8},{16,12},{20,16},{24,20},{28,24},{32,28},{36,32}... | collective-permute-start | bytes 1351688 | tf_op jit(solution)/shard_map/ppermute | solution.py:34
  127.7 6.6 %collective-permute-start.3 = (f32[55,1,2048]{2,1,0:T(1,128)S(1)}, f32[55,1,2048]{2,1,0:T(1,128)S(1)}, u32[]{:S(2)}, u32[]{:S(2)}) collective-permute-start(f32[55,1,2048]{2,1,0:T(1,128)S(1)} %divide_add_fusion), channel_id=1, source_target_pairs={{0,4},{4,8},{8,12},{12,16},{16,20},{20,24},{24,28},{28,32},{32,36}... | collective-permute-start | bytes 1351688 | tf_op jit(solution)/shard_map/ppermute | solution.py:31
  134.3 1.0 slice_bitcast_fusion.4
  135.3 0.1 slice_bitcast_fusion.12
  135.4 1.0 slice_bitcast_fusion.2
  136.4 0.1 slice_bitcast_fusion.10
  136.5 1.1 fusion.161
  137.6 1.1 fusion.163
  138.8 5.2 %collective-permute-done.2 = f32[55,1,2048]{2,1,0:T(1,128)S(1)} collective-permute-done((f32[55,1,2048]{2,1,0:T(1,128)S(1)}, f32[55,1,2048]{2,1,0:T(1,128)S(1)}, u32[]{:S(2)}, u32[]{:S(2)}) %collective-permute-start.2) | collective-permute-done | bytes 450592 | tf_op jit(solution)/shard_map/ppermute | solution.py:34
  144.0 11.2 %collective-permute-done.3 = f32[55,1,2048]{2,1,0:T(1,128)S(1)} collective-permute-done((f32[55,1,2048]{2,1,0:T(1,128)S(1)}, f32[55,1,2048]{2,1,0:T(1,128)S(1)}, u32[]{:S(2)}, u32[]{:S(2)}) %collective-permute-start.3) | collective-permute-done | bytes 450592 | tf_op jit(solution)/shard_map/ppermute | solution.py:31
  155.2 0.9 multiply_bitcast_fusion
  156.1 1.3 pad_maximum_fusion.1
  157.5 0.9 slice_bitcast_fusion.9
  158.4 2.5 %pad_maximum_fusion.2 = f32[4,3,55,1,512]{4,3,2,1,0:T(1,128)} fusion(f32[1,3,55,1,512]{4,3,2,1,0:T(1,128)S(1)} %get-tuple-element.39, f32[1,3,55,1,512]{4,3,2,1,0:T(1,128)S(1)} %get-tuple-element.40, f32[1,3,55,1,512]{4,3,2,1,0:T(1,128)S(1)} %get-tuple-element.41, f32[1,3,55,1,512]{4,3,2,1,0:T(1,128)S(1)} %get-tuple-element.38), kind=kLoop, calls=%fused_computation.8 | loop fusion | flops 1013760 | bytes 2703360 | tf_op jit(solution)/shard_map/stack | solution.py:17
  160.9 3.9 %all-to-all-start = ((f32[4,3,55,1,512]{4,3,2,1,0:T(1,128)}), f32[4,3,55,1,512]{4,3,2,1,0:T(1,128)S(1)}, u32[]{:S(2)}, u32[]{:S(2)}) async-start(f32[4,3,55,1,512]{4,3,2,1,0:T(1,128)} %pad_maximum_fusion.2), calls=%async_computation | async-start | bytes 2703360 | tf_op jit(solution)/shard_map/all_to_all | solution.py:16
  164.8 0.2 fusion.2
  165.2 1.0 fusion.338
  166.2 29.9 %all-to-all-done = f32[4,3,55,1,512]{4,3,2,1,0:T(1,128)S(1)} async-done(((f32[4,3,55,1,512]{4,3,2,1,0:T(1,128)}), f32[4,3,55,1,512]{4,3,2,1,0:T(1,128)S(1)}, u32[]{:S(2)}, u32[]{:S(2)}) %all-to-all-start) | async-done | bytes 1351712 | tf_op jit(solution)/shard_map/all_to_all | solution.py:16
  196.1 1.1 copy-done.1
  197.2 1.5 copy.41
  198.6 1.3 reshape.2097
  199.9 6.3 %multiply_reduce_fusion.1 = f32[512,512]{1,0:T(8,128)S(1)} fusion(f32[3,220,512]{2,1,0:T(8,128)} %reshape.2097, f32[512]{0:T(512)S(1)} %bitcast.226, f32[512]{0:T(512)S(1)} %bitcast.274, f32[512]{0:T(512)S(1)} %bitcast.254, f32[220]{0:T(256)S(1)} %get-tuple-element.135, f32[512]{0:T(512)S(1)} %bitcast.228, f32[512]{0:T(512)S(1)} %bitcast.272, ...), kind=kOutput, calls=%fused_computation.1 | convolution fusion | flops 2084474880 | bytes 2469412 | tf_op jit(solution)/shard_map/qi,kixn->kqxn/dot_general | solution.py:163
  206.3 3.1 %convolution_bitcast_fusion = f32[220,1,512]{2,0,1:T(8,128)S(1)} fusion(f32[512,512]{1,0:T(8,128)S(1)} %multiply_reduce_fusion.1, f32[512]{0:T(512)S(1)} %bitcast.280, f32[512]{0:T(512)S(1)} %bitcast.281, f32[512]{0:T(512)S(1)} %bitcast.282, f32[512]{0:T(512)S(1)} %bitcast.279, f32[512]{0:T(512)S(1)} %bitcast.278, pred[512]{0:T(512)(128)(4,1)S(1)} %copy-done.14, ...), kind=kOutput, calls=%fused_computation.9 | convolution fusion | flops 701628416 | bytes 1582628 | tf_op jit(solution)/shard_map/iq,qxn->ixn/dot_general | solution.py:182
  209.4 1.2 copy.42
  210.6 3.7 %all-to-all-start.1 = ((f32[220,1,512]{2,1,0:T(1,128)}), f32[220,1,512]{2,1,0:T(1,128)S(1)}, u32[]{:S(2)}, u32[]{:S(2)}) async-start(f32[220,1,512]{2,1,0:T(1,128)} %copy.42), calls=%async_computation.1 | async-start | bytes 901120 | tf_op jit(solution)/shard_map/all_to_all | solution.py:183
  214.4 0.2 fusion.340
  214.6 12.8 %all-to-all-done.1 = f32[220,1,512]{2,1,0:T(1,128)S(1)} async-done(((f32[220,1,512]{2,1,0:T(1,128)}), f32[220,1,512]{2,1,0:T(1,128)S(1)}, u32[]{:S(2)}, u32[]{:S(2)}) %all-to-all-start.1) | async-done | bytes 450592 | tf_op jit(solution)/shard_map/all_to_all | solution.py:183
  227.3 1.9 reduce.11
  229.3 1.9 all_to_all.18
  231.2 2.1 copy.43
  233.2 2.1 all_to_all.20
  235.3 1.7 fusion.28
  237.0 1.2 copy.45
  (66 shorter events, 0.9 us)
Async XLA Ops:
  7.2 110.6 %all-gather.3.cloned.1.call-start = ((), (), s32[]{:S(2)}) async-start(), calls=%async_computation.2 | async-start | bytes 2252800 | tf_op jit(solution)/shard_map/all_gather | solution.py:151
  8.7 14.0 %copy-start.5 = (s32[220,9]{0,1:T(8,128)S(1)}, s32[220,9]{0,1:T(8,128)}, u32[]{:S(2)}) copy-start(s32[220,9]{0,1:T(8,128)} %param.15) | copy-start | bytes 23764
  8.7 14.9 %copy-start.8 = (s32[1,2048]{1,0:T(1,128)S(1)}, s32[1,2048]{1,0:T(1,128)}, u32[]{:S(2)}) copy-start(s32[1,2048]{1,0:T(1,128)} %param.13) | copy-start | bytes 24580
  8.8 15.6 %copy-start.6 = (f32[1,2048]{1,0:T(1,128)S(1)}, f32[1,2048]{1,0:T(1,128)}, u32[]{:S(2)}) copy-start(f32[1,2048]{1,0:T(1,128)} %param.12) | copy-start | bytes 24580
  8.8 15.6 %copy-start.9 = (s32[512]{0:T(512)S(1)}, s32[512]{0:T(512)}, u32[]{:S(2)}) copy-start(s32[512]{0:T(512)} %param.17) | copy-start | bytes 6148
  8.8 16.4 %copy-start.10 = (f32[4,9]{1,0:T(4,128)S(1)}, f32[4,9]{1,0:T(4,128)}, u32[]{:S(2)}) copy-start(f32[4,9]{1,0:T(4,128)} %param.14) | copy-start | bytes 436
  9.5 51.8 %collective-permute-start = (f32[2,55,1,2048]{3,0,2,1:T(2,128)S(1)}, f32[2,55,1,2048]{3,0,2,1:T(2,128)}, u32[]{:S(2)}, u32[]{:S(2)}) collective-permute-start(f32[2,55,1,2048]{3,0,2,1:T(2,128)S(1)} %copy.34), channel_id=1, source_target_pairs={{0,4},{4,8},{8,12},{12,16},{16,20},{20,24},{24,28},{28,32},{32,36}... | collective-permute-start | bytes 2703368 | tf_op jit(solution)/shard_map/ppermute | solution.py:31
  20.7 42.3 %collective-permute-start.1 = (f32[2,55,1,2048]{3,0,2,1:T(2,128)S(1)}, f32[2,55,1,2048]{3,0,2,1:T(2,128)}, u32[]{:S(2)}, u32[]{:S(2)}) collective-permute-start(f32[2,55,1,2048]{3,0,2,1:T(2,128)S(1)} %copy.34), channel_id=1, source_target_pairs={{4,0},{8,4},{12,8},{16,12},{20,16},{24,20},{28,24},{32,28},{36,32}... | collective-permute-start | bytes 2703368 | tf_op jit(solution)/shard_map/ppermute | solution.py:34
  71.7 52.0 %copy-start.3 = (f32[55,1,2048]{2,1,0:T(1,128)S(1)}, f32[55,1,2048]{2,1,0:T(1,128)}, u32[]{:S(2)}) copy-start(f32[55,1,2048]{2,1,0:T(1,128)} %param.9) | copy-start | bytes 1351684
  71.7 52.0 %copy-start.4 = (f32[55,1,2048]{2,1,0:T(1,128)S(1)}, f32[55,1,2048]{2,1,0:T(1,128)}, u32[]{:S(2)}) copy-start(f32[55,1,2048]{2,1,0:T(1,128)} %param.10) | copy-start | bytes 1351684
  124.6 11.8 %copy-start = (f32[55,1,2048]{2,1,0:T(1,128)}, f32[55,1,2048]{2,1,0:T(1,128)S(1)}, u32[]{:S(2)}) copy-start(f32[55,1,2048]{2,1,0:T(1,128)S(1)} %divide_add_fusion) | copy-start | bytes 1351684
  124.6 19.4 %collective-permute-start.2 = (f32[55,1,2048]{2,1,0:T(1,128)S(1)}, f32[55,1,2048]{2,1,0:T(1,128)S(1)}, u32[]{:S(2)}, u32[]{:S(2)}) collective-permute-start(f32[55,1,2048]{2,1,0:T(1,128)S(1)} %divide_add_fusion), channel_id=1, source_target_pairs={{4,0},{8,4},{12,8},{16,12},{20,16},{24,20},{28,24},{32,28},{36,32}... | collective-permute-start | bytes 1351688 | tf_op jit(solution)/shard_map/ppermute | solution.py:34
  127.7 27.5 %collective-permute-start.3 = (f32[55,1,2048]{2,1,0:T(1,128)S(1)}, f32[55,1,2048]{2,1,0:T(1,128)S(1)}, u32[]{:S(2)}, u32[]{:S(2)}) collective-permute-start(f32[55,1,2048]{2,1,0:T(1,128)S(1)} %divide_add_fusion), channel_id=1, source_target_pairs={{0,4},{4,8},{8,12},{12,16},{16,20},{20,24},{24,28},{28,32},{32,36}... | collective-permute-start | bytes 1351688 | tf_op jit(solution)/shard_map/ppermute | solution.py:31
  160.9 3.9 %copy-start.7 = (s32[512,9]{0,1:T(8,128)S(1)}, s32[512,9]{0,1:T(8,128)}, u32[]{:S(2)}) copy-start(s32[512,9]{0,1:T(8,128)} %param.16) | copy-start | bytes 55300
  160.9 35.2 %all-to-all-start = ((f32[4,3,55,1,512]{4,3,2,1,0:T(1,128)}), f32[4,3,55,1,512]{4,3,2,1,0:T(1,128)S(1)}, u32[]{:S(2)}, u32[]{:S(2)}) async-start(f32[4,3,55,1,512]{4,3,2,1,0:T(1,128)} %pad_maximum_fusion.2), calls=%async_computation | async-start | bytes 2703360 | tf_op jit(solution)/shard_map/all_to_all | solution.py:16
  196.1 1.1 copy-start.1
  199.9 6.3 %copy-start.11 = (pred[512]{0:T(512)(128)(4,1)S(1)}, pred[512]{0:T(512)(128)(4,1)}, u32[]{:S(2)}) copy-start(pred[512]{0:T(512)(128)(4,1)} %get-tuple-element.10) | copy-start | bytes 1540
  199.9 6.3 %copy-start.12 = (pred[512]{0:T(512)(128)(4,1)S(1)}, pred[512]{0:T(512)(128)(4,1)}, u32[]{:S(2)}) copy-start(pred[512]{0:T(512)(128)(4,1)} %get-tuple-element.11) | copy-start | bytes 1540
  199.9 6.3 %copy-start.13 = (pred[512]{0:T(512)(128)(4,1)S(1)}, pred[512]{0:T(512)(128)(4,1)}, u32[]{:S(2)}) copy-start(pred[512]{0:T(512)(128)(4,1)} %get-tuple-element.12) | copy-start | bytes 1540
  199.9 6.3 %copy-start.14 = (pred[512]{0:T(512)(128)(4,1)S(1)}, pred[512]{0:T(512)(128)(4,1)}, u32[]{:S(2)}) copy-start(pred[512]{0:T(512)(128)(4,1)} %get-tuple-element.13) | copy-start | bytes 1540
  199.9 6.3 %copy-start.15 = (pred[220]{0:T(512)(128)(4,1)S(1)}, pred[220]{0:T(512)(128)(4,1)}, u32[]{:S(2)}) copy-start(pred[220]{0:T(512)(128)(4,1)} %get-tuple-element.108) | copy-start | bytes 664
  199.9 6.3 %copy-start.16 = (pred[220]{0:T(512)(128)(4,1)S(1)}, pred[220]{0:T(512)(128)(4,1)}, u32[]{:S(2)}) copy-start(pred[220]{0:T(512)(128)(4,1)} %get-tuple-element.109) | copy-start | bytes 664
  199.9 6.3 %copy-start.17 = (pred[220]{0:T(512)(128)(4,1)S(1)}, pred[220]{0:T(512)(128)(4,1)}, u32[]{:S(2)}) copy-start(pred[220]{0:T(512)(128)(4,1)} %get-tuple-element.110) | copy-start | bytes 664
  210.6 16.8 %all-to-all-start.1 = ((f32[220,1,512]{2,1,0:T(1,128)}), f32[220,1,512]{2,1,0:T(1,128)S(1)}, u32[]{:S(2)}, u32[]{:S(2)}) async-start(f32[220,1,512]{2,1,0:T(1,128)} %copy.42), calls=%async_computation.1 | async-start | bytes 901120 | tf_op jit(solution)/shard_map/all_to_all | solution.py:183
  229.3 6.1 %copy-start.2 = (f32[55,1,2040]{2,0,1:T(8,128)S(1)}, f32[55,1,2040]{2,0,1:T(8,128)}, u32[]{:S(2)}) copy-start(f32[55,1,2040]{2,0,1:T(8,128)} %get-tuple-element.25) | copy-start | bytes 1346404
Sparse Core Ops, SparseCore 0:
  67.5 50.1 all-gather.2
